TPU v7x, 32 devices: a whole 2x2x4 slice. The times are simulated.
32 devices in a mesh: grp: 2 (over y), stn: 8 (over z, x), tim: 2 (over core).
Axes of the slice: x: 2, y: 2, z: 4, core: 2. Of those that a mesh axis runs over, the one named last changes fastest.
Arguments:
- samples: bfloat16 [256, 32, 8192], P(('grp', 'stn'), 'tim'), parts along dimension 0, may hold values from -6 to 6
- taps: float32 [16, 8192], replicated, may hold values from -1.5 to 1.5
- flags: int32 [256, 32], P('grp'), parts along dimension 0, may hold values from 0 to 1, as said below
- group_owner: int32 [16], P('grp'), parts along dimension 0, may hold values from 0 to 7, each once
Outputs:
- visibility: float32 [16, 128, 2, 128], P(('grp', 'stn'), 'tim'), parts along dimension 0
There are 2 independent parts, one for each index of `grp`. A program takes and returns all parts, laid end to end along the dimension named above; an argument that names none is the same for every part. Nothing has to cross between parts.
Inputs may be any that keep to these rules, and one draw needn't show every extreme that they name: `flags`: each channel's 1 entries form one circular run of consecutive frames, of length 0 to 32. `group_owner`: a permutation of the channel groups.
All inputs are finite; a program needn't handle non-finite values.
Results may differ from a plain program's by a relative error of at most 0.0063.
Values may be sent and summed in bfloat16 or wider, within the bound.
A program may use at most 320 MiB of HBM per device.

v0:
```python
import math

import jax
import jax.numpy as jnp
from jax import lax
from jax.sharding import PartitionSpec as P

BAND_START = 1536


def shifted(block, axis, distance):
    devices = range(lax.axis_size(axis))
    route = [(i - distance, i) for i in devices if i - distance in devices]
    return lax.ppermute(block, axis, route)


def build_planes(fft_len, channel_ids):
    station_block, per_group = channel_ids.shape
    positions = jnp.arange(fft_len, dtype=jnp.int32)
    phase_index = positions[:, None] * (BAND_START + channel_ids.reshape(-1))[None, :] % fft_len
    angle = phase_index.astype(jnp.float32) * (2.0 * math.pi / fft_len)
    amplitude = 1.0 / math.sqrt(fft_len)
    real_part = (jnp.cos(angle) * amplitude).reshape(fft_len, station_block, 1, per_group)
    imag_part = (-jnp.sin(angle) * amplitude).reshape(fft_len, station_block, 1, per_group)
    table = jnp.concatenate([real_part, imag_part], axis=2).astype(jnp.bfloat16)
    return table.reshape(fft_len, station_block * 2 * per_group)


def row_product(left_rows, right_rows):
    return lax.dot_general(
        left_rows, right_rows, (((1,), (1,)), ((), ())), preferred_element_type=jnp.float32
    )


def corner_exchange(outgoing):
    return lax.all_to_all(outgoing, "stn", split_axis=0, concat_axis=0, tiled=True)


def rotate_planes(rows):
    plane_width = rows.shape[1] // 2
    return jnp.concatenate([rows[:, plane_width:], -rows[:, :plane_width]], axis=1)


def channelize(extended, taps, frame_count, owner_channels):
    input_count = extended.shape[0]
    fft_len = extended.shape[2]
    taps_count = taps.shape[0]
    stations, per_group = owner_channels.shape
    flat_samples = extended.reshape(input_count, -1)
    filtered = jnp.zeros((input_count, frame_count, fft_len), jnp.float32)
    for tap_index in range(taps_count):
        window = lax.slice_in_dim(
            flat_samples, tap_index * fft_len, (tap_index + frame_count) * fft_len, axis=1
        )
        window = window.reshape(input_count, frame_count, fft_len)
        filtered = filtered + taps[tap_index][None, None, :] * window.astype(jnp.float32)
    frame_rows = filtered.astype(jnp.bfloat16).reshape(input_count * frame_count, fft_len)
    station_block = math.gcd(stations, max(1, 128 // (2 * per_group)))
    grouped = owner_channels.reshape(stations // station_block, station_block, per_group)

    def transform(block_channels):
        table = build_planes(fft_len, block_channels)
        return jnp.dot(frame_rows, table, preferred_element_type=jnp.float32).astype(jnp.bfloat16)

    spectra = lax.map(transform, grouped)
    spectra = spectra.reshape(
        stations // station_block, input_count, frame_count, station_block, 2, per_group
    )
    spectra = spectra.transpose(0, 3, 1, 4, 2, 5)
    return spectra.reshape(stations, input_count, 2 * frame_count * per_group)


def flag_row(flags, my_group, per_group, first_frame, frame_count):
    valid_mask = lax.dynamic_slice(
        flags, (my_group * per_group, first_frame), (per_group, frame_count)
    )
    plane = valid_mask.T.reshape(-1).astype(jnp.bfloat16)
    return jnp.concatenate([plane, plane])


def per_device(samples, taps, flags, group_owner):
    input_count, spectra_count, fft_len = samples.shape
    taps_count = taps.shape[0]
    stations = lax.axis_size("stn")
    time_devices = lax.axis_size("tim")
    band_width = flags.shape[0]
    per_group = band_width // stations
    station_index = lax.axis_index("stn")
    time_index = lax.axis_index("tim")
    groups = jnp.arange(stations, dtype=jnp.int32)
    owned_group = jnp.sum(
        jnp.where(group_owner[None, :] == groups[:, None], groups[None, :], 0), axis=1
    )
    owner_channels = (
        owned_group[:, None] * per_group + jnp.arange(per_group, dtype=jnp.int32)[None, :]
    )
    my_group = jnp.sum(jnp.where(group_owner == station_index, groups, 0))
    last_frames = samples[:, spectra_count - (taps_count - 1) :, :]
    earlier = shifted(last_frames, "tim", 1)
    extended = jnp.concatenate([earlier, samples], axis=1)
    outgoing = channelize(extended, taps, spectra_count, owner_channels)
    received = corner_exchange(outgoing)
    inputs = received.shape[0] * received.shape[1]
    mask_row = flag_row(flags, my_group, per_group, time_index * spectra_count, spectra_count)
    weighted = (received * mask_row[None, None, :]).reshape(inputs, 2, spectra_count * per_group)
    normaliser = 1.0 / (per_group * spectra_count * time_devices)
    my_rows = inputs // time_devices
    first_row = time_index * my_rows
    all_left = lax.all_gather(weighted, "tim", axis=2, tiled=True).reshape(inputs, -1)
    all_turned = rotate_planes(all_left)
    first_part = lax.dynamic_slice_in_dim(all_left, first_row, my_rows, 0)
    second_part = lax.dynamic_slice_in_dim(all_turned, first_row, my_rows, 0)
    real_part = row_product(first_part, all_left)
    imag_part = row_product(second_part, all_left)
    summed = jnp.stack([real_part, imag_part], axis=1)
    return (summed * normaliser)[None]


def solution(mesh):
    in_specs = (P(("grp", "stn"), "tim", None), P(), P("grp", None), P("grp"))
    out_specs = P(("grp", "stn"), "tim", None, None)
    return jax.shard_map(
        per_device, mesh=mesh, in_specs=in_specs, out_specs=out_specs, check_vma=False
    )
```

profile of v0, /device:TPU:0, one launch (start us, length us, event | category | flops | bytes accessed | tf_op | source)
XLA Modules:
  0.0 297.3 jit_solution(4172526539247322071)
XLA Ops:
  16.7 6.2 %copy.13 = bf16[16,15,8192]{2,1,0:T(8,128)(2,1)} copy(bf16[16,15,8192]{2,0,1:T(8,128)(2,1)} %collective-permute-done) | data formatting | bytes 7864320 | tf_op jit(solution)/shard_map/ppermute | solution.py:14
  22.9 8.8 %pad_maximum_fusion.1 = bf16[16,31,8192]{2,1,0:T(8,128)(2,1)} fusion(bf16[16,16,8192]{2,1,0:T(8,128)(2,1)} %param.6, bf16[16,15,8192]{2,1,0:T(8,128)(2,1)} %copy.13), kind=kLoop, calls=%fused_computation.16 | loop fusion | flops 16252928 | bytes 16252928 | tf_op jit(solution)/shard_map/concatenate | solution.py:100
  31.7 11.2 %copy.17 = bf16[2,8,31,8192]{3,1,2,0:T(8,128)(2,1)} copy(bf16[2,8,31,8192]{3,2,1,0:T(8,128)(2,1)} %bitcast.56) | data formatting | bytes 16252928
  42.9 64.2 %slice_convert_fusion.15 = (f32[16,131072]{1,0:T(8,128)}, f32[16,131072]{1,0:T(8,128)}, f32[16,131072]{1,0:T(8,128)}, f32[16,131072]{1,0:T(8,128)}, f32[16,13107...) fusion(bf16[16,253952]{1,0:T(8,128)(2,1)} %bitcast.54), kind=kLoop, calls=%fused_computation.33 | loop fusion | flops 33554432 | bytes 201326592 | tf_op jit(solution)/shard_map/convert_element_type | solution.py:56
  107.1 6.2 %reshape.249 = f32[256,8192]{1,0:T(8,128)} reshape(f32[16,131072]{1,0:T(8,128)} %get-tuple-element.70) | data formatting | bytes 16777216 | tf_op jit(solution)/shard_map/convert_element_type | solution.py:56
  113.2 6.2 %reshape.250 = f32[256,8192]{1,0:T(8,128)} reshape(f32[16,131072]{1,0:T(8,128)} %get-tuple-element.85) | data formatting | bytes 16777216 | tf_op jit(solution)/shard_map/convert_element_type | solution.py:56
  119.4 6.2 %reshape.251 = f32[256,8192]{1,0:T(8,128)} reshape(f32[16,131072]{1,0:T(8,128)} %get-tuple-element.84) | data formatting | bytes 16777216 | tf_op jit(solution)/shard_map/convert_element_type | solution.py:56
  125.6 6.2 %reshape.252 = f32[256,8192]{1,0:T(8,128)} reshape(f32[16,131072]{1,0:T(8,128)} %get-tuple-element.83) | data formatting | bytes 16777216 | tf_op jit(solution)/shard_map/convert_element_type | solution.py:56
  131.7 6.2 %reshape.253 = f32[256,8192]{1,0:T(8,128)} reshape(f32[16,131072]{1,0:T(8,128)} %get-tuple-element.82) | data formatting | bytes 16777216 | tf_op jit(solution)/shard_map/convert_element_type | solution.py:56
  138.0 6.3 %reshape.254 = f32[256,8192]{1,0:T(8,128)} reshape(f32[16,131072]{1,0:T(8,128)} %get-tuple-element.81) | data formatting | bytes 16777216 | tf_op jit(solution)/shard_map/convert_element_type | solution.py:56
  150.4 6.1 %reshape.256 = f32[256,8192]{1,0:T(8,128)} reshape(f32[16,131072]{1,0:T(8,128)} %get-tuple-element.79) | data formatting | bytes 16777216 | tf_op jit(solution)/shard_map/convert_element_type | solution.py:56
  156.5 6.2 %reshape.257 = f32[256,8192]{1,0:T(8,128)} reshape(f32[16,131072]{1,0:T(8,128)} %get-tuple-element.78) | data formatting | bytes 16777216 | tf_op jit(solution)/shard_map/convert_element_type | solution.py:56
  162.7 6.3 %reshape.258 = f32[256,8192]{1,0:T(8,128)} reshape(f32[16,131072]{1,0:T(8,128)} %get-tuple-element.77) | data formatting | bytes 16777216 | tf_op jit(solution)/shard_map/convert_element_type | solution.py:56
  168.9 6.3 %reshape.259 = f32[256,8192]{1,0:T(8,128)} reshape(f32[16,131072]{1,0:T(8,128)} %get-tuple-element.76) | data formatting | bytes 16777216 | tf_op jit(solution)/shard_map/convert_element_type | solution.py:56
  175.2 6.2 %reshape.260 = f32[256,8192]{1,0:T(8,128)} reshape(f32[16,131072]{1,0:T(8,128)} %get-tuple-element.75) | data formatting | bytes 16777216 | tf_op jit(solution)/shard_map/convert_element_type | solution.py:56
  181.4 6.2 %reshape.261 = f32[256,8192]{1,0:T(8,128)} reshape(f32[16,131072]{1,0:T(8,128)} %get-tuple-element.74) | data formatting | bytes 16777216 | tf_op jit(solution)/shard_map/convert_element_type | solution.py:56
  187.6 6.2 %reshape.262 = f32[256,8192]{1,0:T(8,128)} reshape(f32[16,131072]{1,0:T(8,128)} %get-tuple-element.73) | data formatting | bytes 16777216 | tf_op jit(solution)/shard_map/convert_element_type | solution.py:56
  193.8 6.2 %reshape.263 = f32[256,8192]{1,0:T(8,128)} reshape(f32[16,131072]{1,0:T(8,128)} %get-tuple-element.72) | data formatting | bytes 16777216 | tf_op jit(solution)/shard_map/convert_element_type | solution.py:56
  199.9 6.2 %reshape.264 = f32[256,8192]{1,0:T(8,128)} reshape(f32[16,131072]{1,0:T(8,128)} %get-tuple-element.71) | data formatting | bytes 16777216 | tf_op jit(solution)/shard_map/convert_element_type | solution.py:56
  206.1 43.2 %add_convert_fusion = bf16[256,8192]{1,0:T(8,128)(2,1)} fusion(f32[256,8192]{1,0:T(8,128)} %reshape.264, f32[256,8192]{1,0:T(8,128)} %reshape.263, f32[256,8192]{1,0:T(8,128)} %reshape.262, f32[256,8192]{1,0:T(8,128)} %reshape.261, f32[256,8192]{1,0:T(8,128)} %reshape.260, f32[256,8192]{1,0:T(8,128)} %reshape.259, f32[256,8192]{1,0:T(8,128)} %reshape.258, ...), kind=kLoop, calls=%fused_computation.17 | loop fusion | flops 67108864 | bytes 138936320 | tf_op jit(solution)/shard_map/convert_element_type | solution.py:57
  249.4 26.4 %while.12 = (s32[]{:T(128)}, bf16[2,256,128]{1,2,0:T(8,128)(2,1)S(1)}, s32[2,4,16]{2,1,0:T(4,128)S(1)}, bf16[256,8192]{1,0:T(8,128)(2,1)}, s32[]{:T(128)}) while((s32[]{:T(128)}, bf16[2,256,128]{1,2,0:T(8,128)(2,1)S(1)}, s32[2,4,16]{2,1,0:T(4,128)S(1)}, bf16[256,8192]{1,0:T(8,128)(2,1)}, s32[]{:T(128)}) %tuple.64), condition=%wide.region_2.3_spmd, body=%wide.region_1.2_spmd.sunk | while | flops 547913792 | bytes 12649285 | solution.py:65
  249.4 9.1 %multiply_convert_fusion.3 = (bf16[8192,4,1,16]{0,3,2,1:T(8,128)(2,1)S(1)}, bf16[8192,4,1,16]{0,3,2,1:T(8,128)(2,1)S(1)}) fusion(s32[4,16]{1,0:T(4,128)S(1)} %add_bitcast_fusion.2), kind=kLoop, calls=%fused_computation.8.clone.1 | loop fusion | flops 9961472 | bytes 2097408 | tf_op jit(solution)/shard_map/convert
  262.6 9.1 %multiply_convert_fusion.3 = (bf16[8192,4,1,16]{0,3,2,1:T(8,128)(2,1)S(1)}, bf16[8192,4,1,16]{0,3,2,1:T(8,128)(2,1)S(1)}) fusion(s32[4,16]{1,0:T(4,128)S(1)} %add_bitcast_fusion.2), kind=kLoop, calls=%fused_computation.8.clone.1 | loop fusion | flops 9961472 | bytes 2097408 | tf_op jit(solution)/shard_map/convert
  279.9 6.7 %all-to-all-start = ((bf16[8,16,512]{2,1,0:T(8,128)(2,1)}), bf16[8,16,512]{2,1,0:T(8,128)(2,1)S(1)}, u32[]{:S(2)}, u32[]{:S(2)}) async-start(bf16[8,16,512]{2,1,0:T(8,128)(2,1)} %reshape.246), calls=%async_computation | async-start | bytes 262144 | tf_op jit(solution)/shard_map/all_to_all | solution.py:36
  (46 shorter events, 45.0 us)
Async XLA Ops:
  0.0 11.8 %copy-start.4 = (s32[8]{0:T(128)S(1)}, s32[8]{0:T(128)}, u32[]{:S(2)}) copy-start(s32[8]{0:T(128)} %param.9) | copy-start | bytes 100
  0.0 12.7 %copy-start = (f32[16,8192]{1,0:T(8,128)S(1)}, f32[16,8192]{1,0:T(8,128)}, u32[]{:S(2)}) copy-start(f32[16,8192]{1,0:T(8,128)} %param.7) | copy-start | bytes 1572868
  7.6 9.1 %collective-permute-start = (bf16[16,15,8192]{2,0,1:T(8,128)(2,1)}, bf16[16,15,8192]{2,0,1:T(8,128)(2,1)}, u32[]{:S(2)}, u32[]{:S(2)}) collective-permute-start(bf16[16,15,8192]{2,0,1:T(8,128)(2,1)} %copy.16), channel_id=1, source_target_pairs={{0,1},{2,3},{4,5},{6,7},{8,9},{10,11},{12,13},{14,15},{16,17},{18,... | collective-permute-start | bytes 11796488 | tf_op jit(solution)/shard_map/ppermute | solution.py:14
  206.1 43.2 %copy-start.1 = (bf16[2,256,128]{1,2,0:T(8,128)(2,1)S(1)}, bf16[2,256,128]{1,2,0:T(8,128)(2,1)}, u32[]{:S(2)}) copy-start(bf16[2,256,128]{1,2,0:T(8,128)(2,1)} %custom-call) | copy-start | bytes 393220
  206.1 43.2 %copy-start.2 = (s32[2,4,16]{2,1,0:T(4,128)S(1)}, s32[2,4,16]{2,1,0:T(4,128)}, u32[]{:S(2)}) copy-start(s32[2,4,16]{2,1,0:T(4,128)} %iota_add_fusion) | copy-start | bytes 1540
  249.4 37.2 %copy-start.5 = (s32[8]{0:T(128)S(1)}, s32[8]{0:T(128)}, u32[]{:S(2)}) copy-start(s32[8]{0:T(128)} %param.9) | copy-start | bytes 100
  249.4 38.5 %copy-start.3 = (s32[128,32]{0,1:T(8,128)S(1)}, s32[128,32]{0,1:T(8,128)}, u32[]{:S(2)}) copy-start(s32[128,32]{0,1:T(8,128)} %param.8) | copy-start | bytes 49156
  279.9 14.2 %all-to-all-start = ((bf16[8,16,512]{2,1,0:T(8,128)(2,1)}), bf16[8,16,512]{2,1,0:T(8,128)(2,1)S(1)}, u32[]{:S(2)}, u32[]{:S(2)}) async-start(bf16[8,16,512]{2,1,0:T(8,128)(2,1)} %reshape.246), calls=%async_computation | async-start | bytes 262144 | tf_op jit(solution)/shard_map/all_to_all | solution.py:36
where the time goes:
time: 298 us; the launch traced here: 297 us
  other arithmetic  136 us (46%)
  local copies, waits for them, and re-layouts  130 us (44%)
  starting transfers between devices  10.9 us (4%)
  waiting for transfers between devices  9.54 us (3%)
  matrix products  8.01 us (3%)
    convert_element_type x16, local copies, waits for them, and re-layouts, channelize(): window.astype(jnp.float32)  99 us
    convert_element_type x1, other arithmetic, channelize(): window.astype(jnp.float32)  64.2 us
    convert_element_type x1, other arithmetic, channelize(): filtered.astype(jnp.bfloat16).reshape(input_count * frame_count, fft_len)  43.2 us
    another operation x2, other arithmetic  18.3 us
    unnamed x15, local copies, waits for them, and re-layouts  15.4 us
    concatenate x1, other arithmetic, per_device(): extended = jnp.concatenate([earlier, samples], axis=1)  8.84 us
    dot_general x2, matrix products, transform(): jnp.dot(frame_rows, table, preferred_element_type=jnp.float32)  7.61 us
    all_to_all x1, starting transfers between devices, corner_exchange(): lax.all_to_all(outgoing, 'stn', split_axis=0, concat_axis=0, tiled=True)  6.65 us
  transfers between devices with their start and end apart: 2, of which 2 were waited for; matrix products, arithmetic and copies ran while one was open for 1% of the time, Pallas kernels for 0%

commit v1 on v0

v1 whole, which is shorter than its diff:
```python
import functools
import math

import jax
import jax.numpy as jnp
import numpy as np
from jax import lax
from jax.experimental import pallas as pl
from jax.experimental.pallas import tpu as pltpu
from jax.sharding import PartitionSpec as P

BAND_START = 1536
MESH = pl.DeviceIdType.MESH
LANES = 128
ROW_BLOCK = 64


def phase_tables(fft_len, groups, per_group):
    channels = np.arange(groups * per_group).reshape(groups, per_group) + BAND_START

    def planes(first, second):
        stacked = np.stack([first, second], axis=-2)
        return stacked.reshape(stacked.shape[0], -1).astype(np.float32)

    def angle(positions):
        index = (positions[:, None, None].astype(np.int64) * channels[None]) % fft_len
        return index * (2.0 * math.pi / fft_len)

    outer = angle(np.arange(fft_len // LANES) * LANES)
    inner = angle(np.arange(LANES))
    amplitude = 1.0 / math.sqrt(fft_len)
    outer_same = planes(np.cos(outer), np.cos(outer))
    outer_cross = planes(np.sin(outer), -np.sin(outer))
    inner_own = planes(np.cos(inner) * amplitude, -np.sin(inner) * amplitude)
    inner_swap = planes(-np.sin(inner) * amplitude, np.cos(inner) * amplitude)
    return outer_same, outer_cross, inner_own, inner_swap


def spectra_kernel(samples_ref, taps_ref, same_ref, cross_ref, own_ref, swap_ref, out_ref, wide, rows, table):
    inputs, frames, width = samples_ref.shape
    taps_count = taps_ref.shape[0]
    out_frames = frames + taps_count - 1
    step = pl.program_id(0)

    @pl.when(step == 0)
    def _():
        out_ref[...] = jnp.zeros_like(out_ref)
        rows[out_frames * inputs :, :] = jnp.zeros((rows.shape[0] - out_frames * inputs, width), rows.dtype)

    for chunk in range(width // LANES):
        lanes = slice(chunk * LANES, (chunk + 1) * LANES)
        slot = wide.at[chunk % 2]
        slot[...] = samples_ref[:, :, lanes].astype(jnp.float32).reshape(inputs * frames, LANES)
        weights = [
            jnp.broadcast_to(taps_ref[k : k + 1, lanes], (inputs, LANES)).astype(FILTER_TYPE)
            for k in range(taps_count)
        ]
        frame = [slot[pl.ds(s, inputs, stride=frames), :].astype(FILTER_TYPE) for s in range(frames)]
        for t in range(out_frames):
            terms = []
            for k in range(taps_count):
                s = t - (taps_count - 1) + k
                if 0 <= s < frames:
                    terms.append(weights[k] * frame[s])
            while len(terms) > 1:
                paired = [terms[m] + terms[m + 1] for m in range(0, len(terms) - 1, 2)]
                terms = paired + (terms[-1:] if len(terms) % 2 else [])
            rows[t * inputs : (t + 1) * inputs, lanes] = terms[0].astype(rows.dtype)
        table[lanes, :] = (
            same_ref[chunk : chunk + 1, :] * own_ref[...] + cross_ref[chunk : chunk + 1, :] * swap_ref[...]
        ).astype(table.dtype)
    out_ref[...] += jnp.dot(rows[...], table[...], preferred_element_type=jnp.float32)


FILTER_TYPE = jnp.float32


def partial_spectra(samples, taps, tables):
    inputs, frames, fft_len = samples.shape
    taps_count = taps.shape[0]
    columns = tables[0].shape[1]
    width = min(1024, fft_len)
    row_count = -(-(frames + taps_count - 1) * inputs // 128) * 128
    whole = lambda j: (0, 0)
    return pl.pallas_call(
        spectra_kernel,
        grid=(fft_len // width,),
        in_specs=[
            pl.BlockSpec((inputs, frames, width), lambda j: (0, 0, j)),
            pl.BlockSpec((taps_count, width), lambda j: (0, j)),
            pl.BlockSpec((width // LANES, columns), lambda j: (j, 0)),
            pl.BlockSpec((width // LANES, columns), lambda j: (j, 0)),
            pl.BlockSpec((LANES, columns), whole),
            pl.BlockSpec((LANES, columns), whole),
        ],
        out_specs=pl.BlockSpec((row_count, columns), whole),
        out_shape=jax.ShapeDtypeStruct((row_count, columns), jnp.float32),
        scratch_shapes=[
            pltpu.VMEM((2, inputs * frames, LANES), jnp.float32),
            pltpu.VMEM((row_count, width), jnp.bfloat16),
            pltpu.VMEM((width, columns), jnp.bfloat16),
        ],
        compiler_params=pltpu.CompilerParams(vmem_limit_bytes=48 << 20),
        name="filter_and_transform",
    )(samples, taps, *tables)


def correlate_kernel(
    dims, owner_ref, partial_ref, flags_ref, out_ref,
    earlier, spectra, outgoing, received, products, other,
    near_sem, send_sem, recv_sem, final_sem,
):
    stations, inputs, frames, per_group = dims
    me = lax.axis_index("stn")
    half = lax.axis_index("tim")
    wide = 2 * per_group
    columns = stations * wide
    own_rows = frames * inputs
    per_lane = LANES // wide

    barrier = pltpu.get_barrier_semaphore()
    pl.semaphore_signal(barrier, inc=1, device_id={"tim": 1 - half}, device_id_type=MESH)

    def greet(d, carry):
        pl.semaphore_signal(
            barrier, inc=1, device_id={"stn": lax.rem(me + d, stations)}, device_id_type=MESH
        )
        return carry

    lax.fori_loop(1, stations, greet, 0)

    band = stations * per_group
    channel = lax.broadcasted_iota(jnp.int32, (band, columns), 0)
    column = lax.broadcasted_iota(jnp.int32, (band, columns), 1)
    spread = (channel == column // wide * per_group + column % per_group).astype(jnp.bfloat16)
    flag_rows = flags_ref[...].astype(jnp.float32).astype(jnp.bfloat16)
    valid = jnp.dot(flag_rows, spread, preferred_element_type=jnp.float32)
    valid = jnp.where(half == 0, valid[:frames], valid[frames:])

    lane = lax.broadcasted_iota(jnp.int32, (8, columns), 1)
    target = lane % wide
    for g in range(stations):
        target = jnp.where(lane // wide == g, target + owner_ref[g] * wide, target)
    target = target[:1]

    pl.semaphore_wait(barrier, stations)

    carry_rows = earlier.shape[0]
    near = pltpu.make_async_remote_copy(
        src_ref=partial_ref.at[pl.ds(own_rows, carry_rows), :],
        dst_ref=earlier,
        send_sem=near_sem.at[0],
        recv_sem=near_sem.at[1],
        device_id={"tim": 1 - half},
        device_id_type=MESH,
    )

    @pl.when(half == 0)
    def _():
        near.start()
        spectra[...] = partial_ref[:own_rows, :].astype(jnp.bfloat16)

    @pl.when(half == 1)
    def _():
        near.wait_recv()
        spectra[:carry_rows, :] = (partial_ref[:carry_rows, :] + earlier[...]).astype(jnp.bfloat16)
        spectra[carry_rows:, :] = partial_ref[carry_rows:own_rows, :].astype(jnp.bfloat16)

    weighted = spectra[...].reshape(frames, inputs, columns) * valid.astype(jnp.bfloat16)[:, None, :]
    spectra[...] = weighted.reshape(own_rows, columns)

    slot = lax.broadcasted_iota(jnp.int32, (inputs, LANES), 1) // wide

    def arrange(b, carry):
        row = lax.broadcasted_iota(jnp.int32, (LANES, columns), 0) + b * LANES
        picked = (row == target).astype(jnp.bfloat16)
        block = lax.dot_general(
            spectra[...], picked, (((1,), (1,)), ((), ())), preferred_element_type=jnp.float32
        )
        for r in range(per_lane):
            for quad in range(frames // per_lane):
                total = jnp.zeros((inputs, LANES), jnp.float32)
                for t in range(per_lane):
                    first = (quad * per_lane + t) * inputs
                    piece = block[first : first + inputs, :]
                    if t != r:
                        piece = pltpu.roll(piece, ((t - r) * wide) % LANES, 1)
                    total = jnp.where(slot == t, piece, total)
                outgoing[b * per_lane + r, :, quad * LANES : (quad + 1) * LANES] = total.astype(jnp.bfloat16)
        return carry

    lax.fori_loop(0, stations // per_lane, arrange, 0)

    def turn_copy(d):
        to = lax.rem(me + d, stations)
        return pltpu.make_async_remote_copy(
            src_ref=outgoing.at[to],
            dst_ref=received.at[me],
            send_sem=send_sem.at[d],
            recv_sem=recv_sem.at[d],
            device_id={"stn": to},
            device_id_type=MESH,
        )

    def send(d, carry):
        turn_copy(d).start()
        return carry

    lax.fori_loop(1, stations, send, 0)
    received[me] = outgoing[me]

    def arrive(d, carry):
        turn_copy(d).wait_recv()
        return carry

    lax.fori_loop(1, stations, arrive, 0)

    total_inputs = stations * inputs
    length = frames * wide
    per_block = ROW_BLOCK // inputs
    plane = lax.broadcasted_iota(jnp.int32, (ROW_BLOCK, length), 1) // per_group % 2
    everything = received[...].reshape(total_inputs, length)

    def correlate(b, carry):
        left = received[pl.ds(b * per_block, per_block)].reshape(ROW_BLOCK, length)
        full = left.astype(jnp.float32)
        turned = jnp.where(
            plane == 0, pltpu.roll(full, length - per_group, 1), -pltpu.roll(full, per_group, 1)
        ).astype(jnp.bfloat16)
        both = jnp.concatenate([left, turned], axis=0)
        product = lax.dot_general(
            both, everything, (((1,), (1,)), ((), ())), preferred_element_type=jnp.float32
        )
        products[b] = product.reshape(2, ROW_BLOCK, total_inputs)
        return carry

    lax.fori_loop(0, total_inputs // ROW_BLOCK, correlate, 0)

    mine = out_ref.shape[0]
    last = pltpu.make_async_remote_copy(
        src_ref=products.at[pl.ds((1 - half) * mine, mine)],
        dst_ref=other,
        send_sem=final_sem.at[0],
        recv_sem=final_sem.at[1],
        device_id={"tim": 1 - half},
        device_id_type=MESH,
    )
    last.start()

    def sent(d, carry):
        turn_copy(d).wait_send()
        return carry

    lax.fori_loop(1, stations, sent, 0)

    @pl.when(half == 0)
    def _():
        near.wait_send()

    last.wait()
    normaliser = 1.0 / (per_group * frames * 2)
    out_ref[...] = (products[pl.ds(half * mine, mine)] + other[...]) * normaliser


def correlate(partial, flags, group_owner, stations, inputs, frames, per_group, carry_frames):
    columns = stations * 2 * per_group
    total_inputs = stations * inputs
    blocks = total_inputs // ROW_BLOCK
    length = frames * 2 * per_group
    vmem = pl.BlockSpec(memory_space=pltpu.VMEM)
    return pl.pallas_call(
        functools.partial(correlate_kernel, (stations, inputs, frames, per_group)),
        in_specs=[pl.BlockSpec(memory_space=pltpu.SMEM), vmem, vmem],
        out_specs=vmem,
        out_shape=jax.ShapeDtypeStruct((blocks // 2, 2, ROW_BLOCK, total_inputs), jnp.float32),
        scratch_shapes=[
            pltpu.VMEM((carry_frames * inputs, columns), jnp.float32),
            pltpu.VMEM((frames * inputs, columns), jnp.bfloat16),
            pltpu.VMEM((stations, inputs, length), jnp.bfloat16),
            pltpu.VMEM((stations, inputs, length), jnp.bfloat16),
            pltpu.VMEM((blocks, 2, ROW_BLOCK, total_inputs), jnp.float32),
            pltpu.VMEM((blocks // 2, 2, ROW_BLOCK, total_inputs), jnp.float32),
            pltpu.SemaphoreType.DMA((2,)),
            pltpu.SemaphoreType.DMA((stations,)),
            pltpu.SemaphoreType.DMA((stations,)),
            pltpu.SemaphoreType.DMA((2,)),
        ],
        compiler_params=pltpu.CompilerParams(
            collective_id=0, has_side_effects=True, vmem_limit_bytes=56 << 20
        ),
        name="turn_and_correlate",
    )(group_owner, partial, flags)


def per_device(samples, taps, flags, group_owner):
    inputs, frames, fft_len = samples.shape
    stations = lax.axis_size("stn")
    per_group = flags.shape[0] // stations
    tables = [jnp.asarray(t) for t in phase_tables(fft_len, stations, per_group)]
    partial = partial_spectra(samples, taps, tables)
    blocks = correlate(
        partial, flags.T, group_owner, stations, inputs, frames, per_group, taps.shape[0] - 1
    )
    return blocks.transpose(0, 2, 1, 3).reshape(1, -1, 2, stations * inputs)


def solution(mesh):
    in_specs = (P(("grp", "stn"), "tim", None), P(), P("grp", None), P("grp"))
    out_specs = P(("grp", "stn"), "tim", None, None)
    return jax.shard_map(
        per_device, mesh=mesh, in_specs=in_specs, out_specs=out_specs, check_vma=False
    )
```

time: 298 us -> 39.9 us (0.13)
  other arithmetic: 136 us -> 0 us
  local copies, waits for them, and re-layouts: 130 us -> 9.02 us
  Pallas kernels: 0 us -> 30.5 us
  starting transfers between devices: 10.9 us -> 0 us
  waiting for transfers between devices: 9.54 us -> 0 us
  matrix products: 8.01 us -> 0 us
    convert_element_type x3 -> x0, other arithmetic: 107 us -> none  [the longest x1 64.2 us: channelize(): window.astype(jnp.float32)]
    convert_element_type x17 -> x0, local copies, waits for them, and re-layouts: 99.1 us -> none  [the longest x16 99 us: channelize(): window.astype(jnp.float32)]
    pallas_call x0 -> x2, Pallas kernels: none -> 30.5 us  [the longest x1 16.9 us: partial_spectra(): pl.pallas_call(spectra_kernel, grid=(fft_len // width,), in_specs=[pl.Blo...]
    another operation x2 -> x0, other arithmetic: 18.3 us -> none
    concatenate x4 -> x0, other arithmetic: 9.24 us -> none  [the longest x1 8.84 us: per_device(): extended = jnp.concatenate([earlier, samples], axis=1)]
    dot_general x4 -> x0, matrix products: 8.01 us -> none  [the longest x2 7.61 us: transform(): jnp.dot(frame_rows, table, preferred_element_type=jnp.float32)]
    unnamed x15 -> x14, local copies, waits for them, and re-layouts: 15.4 us -> 7.5 us
    all_to_all x1 -> x0, starting transfers between devices: 6.65 us -> none  [corner_exchange(): lax.all_to_all(outgoing, 'stn', split_axis=0, concat_axis=0, tiled=True)]
  transfers between devices with their start and end apart: 2 -> 0, of which waited for: 2 -> 0; matrix products, arithmetic and copies ran while one was open for 1% -> 0% of each run, Pallas kernels for 0% -> 0%
where the time goes in v1:
time: 39.9 us; the launch traced here: 39.6 us
  Pallas kernels  30.5 us (76%)
  local copies, waits for them, and re-layouts  9.02 us (23%)
    pallas_call x1, Pallas kernels, partial_spectra(): pl.pallas_call(spectra_kernel, grid=(fft_len // width,), in_specs=[pl.Blo...  16.9 us
    pallas_call x1, Pallas kernels, correlate(): pl.pallas_call(functools.partial(correlate_kernel, (stations, inputs, fra...  13.6 us
    unnamed x14, local copies, waits for them, and re-layouts  7.5 us
    transpose x1, local copies, waits for them, and re-layouts, per_device(): return blocks.transpose(0, 2, 1, 3).reshape(1, -1, 2, stations * inputs)  1.52 us

profile of v1, /device:TPU:0, one launch (start us, length us, event | category | flops | bytes accessed | tf_op | source)
XLA Modules:
  0.0 39.6 jit_solution(2329113003342100069)
XLA Ops:
  0.0 0.0 copy-start
  0.0 2.2 %copy-done = bf16[16,16,8192]{2,1,0:T(8,128)(2,1)S(1)} copy-done((bf16[16,16,8192]{2,1,0:T(8,128)(2,1)S(1)}, bf16[16,16,8192]{2,1,0:T(8,128)(2,1)}, u32[]{:S(2)}) %copy-start) | copy-done | bytes 4194328
  2.2 0.0 copy-start.2
  2.2 1.0 %copy-done.2 = f32[16,8192]{1,0:T(8,128)S(1)} copy-done((f32[16,8192]{1,0:T(8,128)S(1)}, f32[16,8192]{1,0:T(8,128)}, u32[]{:S(2)}) %copy-start.2) | copy-done | bytes 524312
  3.2 0.0 copy-start.3
  3.2 0.9 %copy-done.3 = f32[128,256]{1,0:T(8,128)S(1)} copy-done((f32[128,256]{1,0:T(8,128)S(1)}, f32[128,256]{1,0:T(8,128)}, u32[]{:S(2)}) %copy-start.3) | copy-done | bytes 131096
  4.1 0.0 copy-start.4
  4.1 0.9 %copy-done.4 = f32[128,256]{1,0:T(8,128)S(1)} copy-done((f32[128,256]{1,0:T(8,128)S(1)}, f32[128,256]{1,0:T(8,128)}, u32[]{:S(2)}) %copy-start.4) | copy-done | bytes 131096
  5.0 0.0 copy-start.5
  5.0 0.8 %copy-done.5 = f32[64,256]{1,0:T(8,128)S(1)} copy-done((f32[64,256]{1,0:T(8,128)S(1)}, f32[64,256]{1,0:T(8,128)}, u32[]{:S(2)}) %copy-start.5) | copy-done | bytes 65560
  5.9 0.0 copy-start.6
  5.9 0.8 %copy-done.6 = f32[64,256]{1,0:T(8,128)S(1)} copy-done((f32[64,256]{1,0:T(8,128)S(1)}, f32[64,256]{1,0:T(8,128)}, u32[]{:S(2)}) %copy-start.6) | copy-done | bytes 65560
  6.7 16.9 %filter_and_transform.1.partial_ref = f32[512,256]{1,0:T(8,128)S(1)} custom-call(bf16[16,16,8192]{2,1,0:T(8,128)(2,1)S(1)} %copy-done, f32[16,8192]{1,0:T(8,128)S(1)} %copy-done.2, f32[64,256]{1,0:T(8,128)S(1)} %copy-done.6, f32[64,256]{1,0:T(8,128)S(1)} %copy-done.5, f32[128,256]{1,0:T(8,128)S(1)} %copy-done.4, f32[128,256]{1,0:T(8,128)S(1)} %copy-done.3), custom_call_target="tpu_custom_call" | custom-call | tf_op jit(solution)/shard_map/filter_and_transform/pallas_call | solution.py:85
  23.6 0.0 copy-start.1
  23.6 0.8 %copy-done.1 = f32[512,256]{1,0:T(8,128)} copy-done((f32[512,256]{1,0:T(8,128)}, f32[512,256]{1,0:T(8,128)S(1)}, u32[]{:S(2)}) %copy-start.1) | copy-done | bytes 524312
  24.4 13.6 %turn_and_correlate.1 = f32[1,2,64,128]{3,2,1,0:T(8,128)} custom-call(s32[8]{0:T(128)} %owner_ref.1, f32[512,256]{1,0:T(8,128)} %copy-done.1, s32[32,128]{1,0:T(8,128)} %bitcast.3), custom_call_target="tpu_custom_call" | custom-call | tf_op jit(solution)/shard_map/turn_and_correlate/pallas_call | solution.py:271
  38.0 1.5 %copy.9 = f32[1,64,2,128]{3,2,1,0:T(2,128)} copy(f32[1,64,2,128]{3,1,2,0:T(8,128)} %bitcast.2) | data formatting | bytes 131072 | tf_op jit(solution)/shard_map/transpose | solution.py:304
Async XLA Ops:
  0.0 2.2 %copy-start = (bf16[16,16,8192]{2,1,0:T(8,128)(2,1)S(1)}, bf16[16,16,8192]{2,1,0:T(8,128)(2,1)}, u32[]{:S(2)}) copy-start(bf16[16,16,8192]{2,1,0:T(8,128)(2,1)} %samples_ref.1) | copy-start | bytes 12582916
  2.2 1.0 %copy-start.2 = (f32[16,8192]{1,0:T(8,128)S(1)}, f32[16,8192]{1,0:T(8,128)}, u32[]{:S(2)}) copy-start(f32[16,8192]{1,0:T(8,128)} %taps_ref.1) | copy-start | bytes 1572868
  3.2 0.9 %copy-start.3 = (f32[128,256]{1,0:T(8,128)S(1)}, f32[128,256]{1,0:T(8,128)}, u32[]{:S(2)}) copy-start(f32[128,256]{1,0:T(8,128)} %constant.11.clone.swap_ref) | copy-start | bytes 393220
  4.1 0.9 %copy-start.4 = (f32[128,256]{1,0:T(8,128)S(1)}, f32[128,256]{1,0:T(8,128)}, u32[]{:S(2)}) copy-start(f32[128,256]{1,0:T(8,128)} %constant.10.clone.own_ref) | copy-start | bytes 393220
  5.0 0.8 %copy-start.5 = (f32[64,256]{1,0:T(8,128)S(1)}, f32[64,256]{1,0:T(8,128)}, u32[]{:S(2)}) copy-start(f32[64,256]{1,0:T(8,128)} %constant.9.clone.cross_ref) | copy-start | bytes 196612
  5.9 0.8 %copy-start.6 = (f32[64,256]{1,0:T(8,128)S(1)}, f32[64,256]{1,0:T(8,128)}, u32[]{:S(2)}) copy-start(f32[64,256]{1,0:T(8,128)} %constant.8.clone.same_ref) | copy-start | bytes 196612
  23.6 0.8 %copy-start.1 = (f32[512,256]{1,0:T(8,128)}, f32[512,256]{1,0:T(8,128)S(1)}, u32[]{:S(2)}) copy-start(f32[512,256]{1,0:T(8,128)S(1)} %filter_and_transform.1.partial_ref) | copy-start | bytes 1572868

commit v2 on v0

v2 whole, which is shorter than its diff:
```python
import functools
import math

import jax
import jax.numpy as jnp
import numpy as np
from jax import lax
from jax.experimental import pallas as pl
from jax.experimental.pallas import tpu as pltpu
from jax.sharding import PartitionSpec as P

BAND_START = 1536
MESH = pl.DeviceIdType.MESH
LANES = 128
ROW_BLOCK = 64
STEP_WIDTH = 1024
TABLE_LIMIT = 8 << 20


def phase_tables(fft_len, groups, per_group):
    channels = np.arange(groups * per_group).reshape(groups, per_group) + BAND_START

    def planes(first, second):
        stacked = np.stack([first, second], axis=-2)
        return stacked.reshape(stacked.shape[0], -1).astype(np.float32)

    def angle(positions):
        index = (positions[:, None, None].astype(np.int64) * channels[None]) % fft_len
        return index * (2.0 * math.pi / fft_len)

    outer = angle(np.arange(fft_len // LANES) * LANES)
    inner = angle(np.arange(LANES))
    amplitude = 1.0 / math.sqrt(fft_len)
    outer_same = planes(np.cos(outer), np.cos(outer))
    outer_cross = planes(np.sin(outer), -np.sin(outer))
    inner_own = planes(np.cos(inner) * amplitude, -np.sin(inner) * amplitude)
    inner_swap = planes(-np.sin(inner) * amplitude, np.cos(inner) * amplitude)
    return outer_same, outer_cross, inner_own, inner_swap


def filter_chunk(samples_ref, taps_ref, wide, rows, lanes, to):
    inputs, frames, _ = samples_ref.shape
    taps_count = taps_ref.shape[0]
    wide[...] = samples_ref[:, :, lanes].astype(jnp.float32).reshape(inputs * frames, LANES)
    weights = [
        jnp.broadcast_to(taps_ref[k : k + 1, lanes], (inputs, LANES)).astype(jnp.bfloat16)
        for k in range(taps_count)
    ]
    frame = [wide[pl.ds(s, inputs, stride=frames), :].astype(jnp.bfloat16) for s in range(frames)]
    for t in range(frames + taps_count - 1):
        first = t - (taps_count - 1)
        terms = [weights[k] * frame[first + k] for k in range(taps_count) if 0 <= first + k < frames]
        while len(terms) > 1:
            paired = [terms[m] + terms[m + 1] for m in range(0, len(terms) - 1, 2)]
            terms = paired + (terms[-1:] if len(terms) % 2 else [])
        rows[t * inputs : (t + 1) * inputs, to] = terms[0]


def kernel(
    dims, owner_ref, samples_ref, taps_ref, same_ref, cross_ref, own_ref, swap_ref, flags_ref, out_ref,
    wide, rows, table, total, valid, later, earlier, spectra, outgoing, received, products, other,
    near_sem, send_sem, recv_sem, final_sem,
):
    stations, per_group, steps, span = dims
    inputs, frames, width = samples_ref.shape
    carry_rows = later.shape[0]
    own_rows = frames * inputs
    group_width = 2 * per_group
    columns = stations * group_width
    per_lane = LANES // group_width
    step = pl.program_id(0)
    me = lax.axis_index("stn")
    half = lax.axis_index("tim")
    barrier = pltpu.get_barrier_semaphore()

    @pl.when(step == 0)
    def _():
        pl.semaphore_signal(barrier, inc=1, device_id={"tim": 1 - half}, device_id_type=MESH)

        def greet(d, carry):
            pl.semaphore_signal(
                barrier, inc=1, device_id={"stn": lax.rem(me + d, stations)}, device_id_type=MESH
            )
            return carry

        lax.fori_loop(1, stations, greet, 0)
        if span < steps:
            total[...] = jnp.zeros_like(total)
        band = stations * per_group
        channel = lax.broadcasted_iota(jnp.int32, (band, columns), 0)
        column = lax.broadcasted_iota(jnp.int32, (band, columns), 1)
        spread = (channel == column // group_width * per_group + column % per_group).astype(jnp.bfloat16)
        flag_rows = flags_ref[...].astype(jnp.float32).astype(jnp.bfloat16)
        both = jnp.dot(flag_rows, spread, preferred_element_type=jnp.float32)
        valid[...] = jnp.where(half == 0, both[:frames], both[frames:])

    place = lax.rem(step, span) * width

    def chunk(c, carry):
        lanes = pl.ds(pl.multiple_of(c * LANES, LANES), LANES)
        to = pl.ds(pl.multiple_of(place + c * LANES, LANES), LANES)
        filter_chunk(samples_ref, taps_ref, wide, rows, lanes, to)
        table[to, :] = (
            same_ref[pl.ds(c, 1), :] * own_ref[...] + cross_ref[pl.ds(c, 1), :] * swap_ref[...]
        ).astype(table.dtype)
        return carry

    lax.fori_loop(0, width // LANES, chunk, 0)

    def transform(low, high):
        return jnp.dot(rows[low:high, :], table[...], preferred_element_type=jnp.float32)

    if span < steps:

        @pl.when(jnp.logical_and(lax.rem(step, span) == span - 1, step < steps - 1))
        def _():
            total[...] += transform(0, own_rows + carry_rows)

    @pl.when(step == steps - 1)
    def _():
        def finished(low, high):
            result = transform(low, high)
            return result + total[low:high, :] if span < steps else result

        later[...] = finished(own_rows, own_rows + carry_rows)
        pl.semaphore_wait(barrier, stations)
        near = pltpu.make_async_remote_copy(
            src_ref=later,
            dst_ref=earlier,
            send_sem=near_sem.at[0],
            recv_sem=near_sem.at[1],
            device_id={"tim": 1 - half},
            device_id_type=MESH,
        )

        @pl.when(half == 0)
        def _():
            near.start()

        mine = finished(0, own_rows)
        lane = lax.broadcasted_iota(jnp.int32, (8, columns), 1)
        target = lane % group_width
        for g in range(stations):
            target = jnp.where(lane // group_width == g, target + owner_ref[g] * group_width, target)
        target = target[:1]
        mask = valid[...].astype(jnp.bfloat16)

        def weigh(values, low, high):
            count = high - low
            shaped = values.astype(jnp.bfloat16).reshape(count, inputs, columns)
            spectra[low * inputs : high * inputs, :] = (shaped * mask[low:high, None, :]).reshape(
                count * inputs, columns
            )

        @pl.when(half == 0)
        def _():
            weigh(mine, 0, frames)

        @pl.when(half == 1)
        def _():
            near.wait_recv()
            carried = carry_rows // inputs
            weigh(mine[:carry_rows] + earlier[...], 0, carried)
            weigh(mine[carry_rows:], carried, frames)

        slot = lax.broadcasted_iota(jnp.int32, (inputs, LANES), 1) // group_width

        def turn_copy(d):
            to = lax.rem(me + d, stations)
            return pltpu.make_async_remote_copy(
                src_ref=outgoing.at[to],
                dst_ref=received.at[me],
                send_sem=send_sem.at[d],
                recv_sem=recv_sem.at[d],
                device_id={"stn": to},
                device_id_type=MESH,
            )

        def arrange(b, carry):
            row = lax.broadcasted_iota(jnp.int32, (LANES, columns), 0) + b * LANES
            picked = (row == target).astype(jnp.bfloat16)
            block = lax.dot_general(
                spectra[...], picked, (((1,), (1,)), ((), ())), preferred_element_type=jnp.float32
            )
            for r in range(per_lane):
                for quad in range(frames // per_lane):
                    joined = jnp.zeros((inputs, LANES), jnp.float32)
                    for t in range(per_lane):
                        first = (quad * per_lane + t) * inputs
                        piece = block[first : first + inputs, :]
                        if t != r:
                            piece = pltpu.roll(piece, ((t - r) * group_width) % LANES, 1)
                        joined = jnp.where(slot == t, piece, joined)
                    outgoing[b * per_lane + r, :, quad * LANES : (quad + 1) * LANES] = joined.astype(
                        jnp.bfloat16
                    )
            return carry

        lax.fori_loop(0, stations // per_lane, arrange, 0)

        def send(d, carry):
            turn_copy(d).start()
            return carry

        lax.fori_loop(1, stations, send, 0)
        received[me] = outgoing[me]

        def arrive(d, carry):
            turn_copy(d).wait_recv()
            return carry

        lax.fori_loop(1, stations, arrive, 0)

        total_inputs = stations * inputs
        length = frames * group_width
        per_block = ROW_BLOCK // inputs
        plane = lax.broadcasted_iota(jnp.int32, (ROW_BLOCK, length), 1) // per_group % 2
        everything = received[...].reshape(total_inputs, length)

        def correlate(b, carry):
            left = received[pl.ds(b * per_block, per_block)].reshape(ROW_BLOCK, length)
            full = left.astype(jnp.float32)
            turned = jnp.where(
                plane == 0, pltpu.roll(full, length - per_group, 1), -pltpu.roll(full, per_group, 1)
            ).astype(jnp.bfloat16)
            pair = jnp.concatenate([left, turned], axis=0)
            product = lax.dot_general(
                pair, everything, (((1,), (1,)), ((), ())), preferred_element_type=jnp.float32
            )
            products[b] = product.reshape(2, ROW_BLOCK, total_inputs)
            return carry

        blocks = out_ref.shape[0]
        last = pltpu.make_async_remote_copy(
            src_ref=products.at[pl.ds((1 - half) * blocks, blocks)],
            dst_ref=other,
            send_sem=final_sem.at[0],
            recv_sem=final_sem.at[1],
            device_id={"tim": 1 - half},
            device_id_type=MESH,
        )
        lax.fori_loop((1 - half) * blocks, (2 - half) * blocks, correlate, 0)
        last.start()
        lax.fori_loop(half * blocks, (1 + half) * blocks, correlate, 0)

        def sent(d, carry):
            turn_copy(d).wait_send()
            return carry

        lax.fori_loop(1, stations, sent, 0)

        @pl.when(half == 0)
        def _():
            near.wait_send()

        last.wait()
        normaliser = 1.0 / (per_group * frames * 2)
        out_ref[...] = (products[pl.ds(half * blocks, blocks)] + other[...]) * normaliser


def per_device(samples, taps, flags, group_owner):
    inputs, frames, fft_len = samples.shape
    taps_count = taps.shape[0]
    stations = lax.axis_size("stn")
    band = flags.shape[0]
    per_group = band // stations
    columns = 2 * band
    total_inputs = stations * inputs
    blocks = total_inputs // ROW_BLOCK
    length = frames * 2 * per_group
    width = min(STEP_WIDTH, fft_len)
    steps = fft_len // width
    span = steps
    while span > 1 and span * width * columns * 2 > TABLE_LIMIT:
        span //= 2
    carry_rows = (taps_count - 1) * inputs
    row_count = frames * inputs + carry_rows
    total_shape = (row_count, columns) if span < steps else (8, LANES)
    tables = [jnp.asarray(t) for t in phase_tables(fft_len, stations, per_group)]
    per_step = width // LANES
    whole = lambda j: (0, 0)
    result = pl.pallas_call(
        functools.partial(kernel, (stations, per_group, steps, span)),
        grid=(steps,),
        in_specs=[
            pl.BlockSpec(memory_space=pltpu.SMEM),
            pl.BlockSpec((inputs, frames, width), lambda j: (0, 0, j)),
            pl.BlockSpec((taps_count, width), lambda j: (0, j)),
            pl.BlockSpec((per_step, columns), lambda j: (j, 0)),
            pl.BlockSpec((per_step, columns), lambda j: (j, 0)),
            pl.BlockSpec((LANES, columns), whole),
            pl.BlockSpec((LANES, columns), whole),
            pl.BlockSpec((flags.shape[1], band), whole),
        ],
        out_specs=pl.BlockSpec((blocks // 2, 2, ROW_BLOCK, total_inputs), lambda j: (0, 0, 0, 0)),
        out_shape=jax.ShapeDtypeStruct((blocks // 2, 2, ROW_BLOCK, total_inputs), jnp.float32),
        scratch_shapes=[
            pltpu.VMEM((inputs * frames, LANES), jnp.float32),
            pltpu.VMEM((row_count, span * width), jnp.bfloat16),
            pltpu.VMEM((span * width, columns), jnp.bfloat16),
            pltpu.VMEM(total_shape, jnp.float32),
            pltpu.VMEM((frames, columns), jnp.float32),
            pltpu.VMEM((carry_rows, columns), jnp.float32),
            pltpu.VMEM((carry_rows, columns), jnp.float32),
            pltpu.VMEM((frames * inputs, columns), jnp.bfloat16),
            pltpu.VMEM((stations, inputs, length), jnp.bfloat16),
            pltpu.VMEM((stations, inputs, length), jnp.bfloat16),
            pltpu.VMEM((blocks, 2, ROW_BLOCK, total_inputs), jnp.float32),
            pltpu.VMEM((blocks // 2, 2, ROW_BLOCK, total_inputs), jnp.float32),
            pltpu.SemaphoreType.DMA((2,)),
            pltpu.SemaphoreType.DMA((stations,)),
            pltpu.SemaphoreType.DMA((stations,)),
            pltpu.SemaphoreType.DMA((2,)),
        ],
        compiler_params=pltpu.CompilerParams(
            collective_id=0, has_side_effects=True, vmem_limit_bytes=60 << 20
        ),
        name="correlator",
    )(group_owner, samples, taps, *tables, flags.T)
    return result.transpose(0, 2, 1, 3).reshape(1, -1, 2, total_inputs)


def solution(mesh):
    in_specs = (P(("grp", "stn"), "tim", None), P(), P("grp", None), P("grp"))
    out_specs = P(("grp", "stn"), "tim", None, None)
    return jax.shard_map(
        per_device, mesh=mesh, in_specs=in_specs, out_specs=out_specs, check_vma=False
    )
```

time: 298 us -> 27.5 us (0.09)
  other arithmetic: 136 us -> 0 us
  local copies, waits for them, and re-layouts: 130 us -> 1.52 us
  Pallas kernels: 0 us -> 25.8 us
  starting transfers between devices: 10.9 us -> 0 us
  waiting for transfers between devices: 9.54 us -> 0 us
  matrix products: 8.01 us -> 0 us
    convert_element_type x3 -> x0, other arithmetic: 107 us -> none  [the longest x1 64.2 us: channelize(): window.astype(jnp.float32)]
    convert_element_type x17 -> x0, local copies, waits for them, and re-layouts: 99.1 us -> none  [the longest x16 99 us: channelize(): window.astype(jnp.float32)]
    pallas_call x0 -> x1, Pallas kernels: none -> 25.8 us  [per_device(): pl.pallas_call(functools.partial(kernel, (stations, per_group, steps, spa...]
    another operation x2 -> x0, other arithmetic: 18.3 us -> none
    unnamed x15 -> x0, local copies, waits for them, and re-layouts: 15.4 us -> none
    concatenate x4 -> x0, other arithmetic: 9.24 us -> none  [the longest x1 8.84 us: per_device(): extended = jnp.concatenate([earlier, samples], axis=1)]
    dot_general x4 -> x0, matrix products: 8.01 us -> none  [the longest x2 7.61 us: transform(): jnp.dot(frame_rows, table, preferred_element_type=jnp.float32)]
    all_to_all x1 -> x0, starting transfers between devices: 6.65 us -> none  [corner_exchange(): lax.all_to_all(outgoing, 'stn', split_axis=0, concat_axis=0, tiled=True)]
  transfers between devices with their start and end apart: 2 -> 0, of which waited for: 2 -> 0; matrix products, arithmetic and copies ran while one was open for 1% -> 0% of each run, Pallas kernels for 0% -> 0%
where the time goes in v2:
time: 27.5 us; the launch traced here: 27.4 us
  Pallas kernels  25.8 us (94%)
  local copies, waits for them, and re-layouts  1.52 us (6%)
    pallas_call x1, Pallas kernels, per_device(): pl.pallas_call(functools.partial(kernel, (stations, per_group, steps, spa...  25.8 us
    transpose x1, local copies, waits for them, and re-layouts, per_device(): return result.transpose(0, 2, 1, 3).reshape(1, -1, 2, total_inputs)  1.52 us

profile of v2, /device:TPU:0, one launch (start us, length us, event | category | flops | bytes accessed | tf_op | source)
XLA Modules:
  0.0 27.4 jit_solution(8097803603276855672)
XLA Ops:
  0.0 25.8 %correlator.1 = f32[1,2,64,128]{3,2,1,0:T(8,128)} custom-call(s32[8]{0:T(128)} %owner_ref.1, bf16[16,16,8192]{2,1,0:T(8,128)(2,1)} %samples_ref.1, f32[16,8192]{1,0:T(8,128)} %taps_ref.1, f32[64,256]{1,0:T(8,128)} %constant.8.clone.same_ref, f32[64,256]{1,0:T(8,128)} %constant.9.clone.cross_ref, f32[128,256]{1,0:T(8,128)} %constant.10.clone.own_ref, ...), custom_call_target="tpu_custom_call" | custom-call | tf_op jit(solution)/shard_map/correlator/pallas_call | solution.py:282
  25.8 1.5 %copy.9 = f32[1,64,2,128]{3,2,1,0:T(2,128)} copy(f32[1,64,2,128]{3,1,2,0:T(8,128)} %bitcast.2) | data formatting | bytes 131072 | tf_op jit(solution)/shard_map/transpose | solution.py:320

commit v3 on v2

--- a/solution.py
+++ b/solution.py
@@ -96,16 +96,39 @@
 
     place = lax.rem(step, span) * width
 
-    def chunk(c, carry):
-        lanes = pl.ds(pl.multiple_of(c * LANES, LANES), LANES)
-        to = pl.ds(pl.multiple_of(place + c * LANES, LANES), LANES)
-        filter_chunk(samples_ref, taps_ref, wide, rows, lanes, to)
-        table[to, :] = (
+    def chunks(fill):
+        def chunk(c, carry):
+            lanes = pl.ds(pl.multiple_of(c * LANES, LANES), LANES)
+            filter_chunk(samples_ref, taps_ref, wide, rows, lanes, pl.ds(pl.multiple_of(place + c * LANES, LANES), LANES))
+            fill(c, place + c * LANES)
+            return carry
+
+        lax.fori_loop(0, width // LANES, chunk, 0, unroll=4)
+
+    def build(c, to):
+        table[pl.ds(pl.multiple_of(to, LANES), LANES), :] = (
             same_ref[pl.ds(c, 1), :] * own_ref[...] + cross_ref[pl.ds(c, 1), :] * swap_ref[...]
         ).astype(table.dtype)
-        return carry
-
-    lax.fori_loop(0, width // LANES, chunk, 0)
+
+    if span == steps and steps % 2 == 0:
+        middle = table.shape[0] // 2
+        lane_column = lax.broadcasted_iota(jnp.int32, (LANES, columns), 1)
+        bins = BAND_START + lane_column // group_width * per_group + lane_column % per_group
+        sign = (1 - 2 * (bins % 2)).astype(jnp.float32).astype(table.dtype)
+
+        def mirror(c, to):
+            source = table[pl.ds(pl.multiple_of(to - middle, LANES), LANES), :]
+            table[pl.ds(pl.multiple_of(to, LANES), LANES), :] = source * sign
+
+        @pl.when(step < steps // 2)
+        def _():
+            chunks(build)
+
+        @pl.when(step >= steps // 2)
+        def _():
+            chunks(mirror)
+    else:
+        chunks(build)
 
     def transform(low, high):
         return jnp.dot(rows[low:high, :], table[...], preferred_element_type=jnp.float32)

time: 27.5 us -> 26.9 us (0.978)
  Pallas kernels: 25.8 us -> 25.1 us
    pallas_call x1, Pallas kernels: 25.8 us -> 25.1 us  [per_device(): pl.pallas_call(functools.partial(kernel, (stations, per_group, steps, spa...]
where the time goes in v3:
time: 26.9 us; the launch traced here: 26.6 us
  Pallas kernels  25.1 us (93%)
  local copies, waits for them, and re-layouts  1.52 us (6%)
    pallas_call x1, Pallas kernels, per_device(): pl.pallas_call(functools.partial(kernel, (stations, per_group, steps, spa...  25.1 us
    transpose x1, local copies, waits for them, and re-layouts, per_device(): return result.transpose(0, 2, 1, 3).reshape(1, -1, 2, total_inputs)  1.52 us

profile of v3, /device:TPU:0, one launch (start us, length us, event | category | flops | bytes accessed | tf_op | source)
XLA Modules:
  0.0 26.6 jit_solution(6053702795647985127)
XLA Ops:
  0.0 25.1 %correlator.1 = f32[1,2,64,128]{3,2,1,0:T(8,128)} custom-call(s32[8]{0:T(128)} %owner_ref.1, bf16[16,16,8192]{2,1,0:T(8,128)(2,1)} %samples_ref.1, f32[16,8192]{1,0:T(8,128)} %taps_ref.1, f32[64,256]{1,0:T(8,128)} %constant.8.clone.same_ref, f32[64,256]{1,0:T(8,128)} %constant.9.clone.cross_ref, f32[128,256]{1,0:T(8,128)} %constant.10.clone.own_ref, ...), custom_call_target="tpu_custom_call" | custom-call | tf_op jit(solution)/shard_map/correlator/pallas_call | solution.py:305
  25.1 1.5 %copy.9 = f32[1,64,2,128]{3,2,1,0:T(2,128)} copy(f32[1,64,2,128]{3,1,2,0:T(8,128)} %bitcast.2) | data formatting | bytes 131072 | tf_op jit(solution)/shard_map/transpose | solution.py:343

commit v4 on v3

--- a/solution.py
+++ b/solution.py
@@ -199,7 +199,8 @@
                 device_id_type=MESH,
             )
 
-        def arrange(b, carry):
+        def arrange(turn, carry):
+            b = lax.rem(turn + 1 + me // per_lane, stations // per_lane)
             row = lax.broadcasted_iota(jnp.int32, (LANES, columns), 0) + b * LANES
             picked = (row == target).astype(jnp.bfloat16)
             block = lax.dot_general(
@@ -217,15 +218,17 @@
                     outgoing[b * per_lane + r, :, quad * LANES : (quad + 1) * LANES] = joined.astype(
                         jnp.bfloat16
                     )
+            for r in range(per_lane):
+                to = b * per_lane + r
+
+                @pl.when(to != me)
+                def _():
+                    turn_copy(lax.rem(to - me + stations, stations)).start()
+
             return carry
 
         lax.fori_loop(0, stations // per_lane, arrange, 0)
 
-        def send(d, carry):
-            turn_copy(d).start()
-            return carry
-
-        lax.fori_loop(1, stations, send, 0)
         received[me] = outgoing[me]
 
         def arrive(d, carry):

time: 26.9 us -> 26.6 us (0.989)
  Pallas kernels: 25.1 us -> 24.8 us
    pallas_call x1, Pallas kernels: 25.1 us -> 24.8 us  [per_device(): pl.pallas_call(functools.partial(kernel, (stations, per_group, steps, spa...]
where the time goes in v4:
time: 26.6 us; the launch traced here: 26.4 us
  Pallas kernels  24.8 us (93%)
  local copies, waits for them, and re-layouts  1.52 us (6%)
    pallas_call x1, Pallas kernels, per_device(): pl.pallas_call(functools.partial(kernel, (stations, per_group, steps, spa...  24.8 us
    transpose x1, local copies, waits for them, and re-layouts, per_device(): return result.transpose(0, 2, 1, 3).reshape(1, -1, 2, total_inputs)  1.52 us

profile of v4, /device:TPU:0, one launch (start us, length us, event | category | flops | bytes accessed | tf_op | source)
XLA Modules:
  0.0 26.4 jit_solution(6249207434700422038)
XLA Ops:
  0.0 24.8 %correlator.1 = f32[1,2,64,128]{3,2,1,0:T(8,128)} custom-call(s32[8]{0:T(128)} %owner_ref.1, bf16[16,16,8192]{2,1,0:T(8,128)(2,1)} %samples_ref.1, f32[16,8192]{1,0:T(8,128)} %taps_ref.1, f32[64,256]{1,0:T(8,128)} %constant.8.clone.same_ref, f32[64,256]{1,0:T(8,128)} %constant.9.clone.cross_ref, f32[128,256]{1,0:T(8,128)} %constant.10.clone.own_ref, ...), custom_call_target="tpu_custom_call" | custom-call | tf_op jit(solution)/shard_map/correlator/pallas_call | solution.py:308
  24.8 1.5 %copy.9 = f32[1,64,2,128]{3,2,1,0:T(2,128)} copy(f32[1,64,2,128]{3,1,2,0:T(8,128)} %bitcast.2) | data formatting | bytes 131072 | tf_op jit(solution)/shard_map/transpose | solution.py:346
